TPU v7x, 32 devices: a whole 2x2x4 slice. The times are simulated.
32 devices in a mesh: row: 4 (over y, x), col: 8 (over z, core).
Axes of the slice: x: 2, y: 2, z: 4, core: 2. Of those that a mesh axis runs over, the one named last changes fastest.
Arguments:
- anc_inverse: float32 [10240, 10240], P('row', 'col'), may hold values from -0.0625 to 0.0625
- lower_anc: float32 [10240, 3, 384], P('col', None, 'row'), may hold values from -1.5 to 1.5
- upper_anc: float32 [10240, 3, 384], P('row', None, 'col'), may hold values from -0.75 to 0.75
- lower_edge: float32 [2, 384, 384], replicated, may hold values from -0.3125 to 0.3125
- upper_edge: float32 [2, 384, 384], replicated, may hold values from -0.3125 to 0.3125
- diag_inverse: float32 [3, 384, 384], replicated, may hold values from -6 to 6
- tile_mask: int32 [3, 80, 3], replicated, may hold values 0 or 1
Outputs:
- x_blocks: float32 [10240, 3, 384], P(('row', 'col'))
- y_blocks: float32 [8, 4, 320, 3, 384], P('col', 'row')
- z_blocks: float32 [3, 384, 384], P(None, 'row', 'col')
- cross_blocks: float32 [2, 2, 384, 384], P(None, None, 'row', 'col')
All inputs are finite; a program needn't handle non-finite values.
Results may differ from a plain program's by a relative error of at most 0.0001.
Values sent between devices are 32-bit elements; how exact they have to be, the bound alone decides.
A program may use at most 128 MiB of HBM per device.

v0:
```python
import jax
import jax.numpy as jnp
from jax import lax
from jax.sharding import PartitionSpec as P

W = 384
BLK = 128
SUPER = 3
precise = lax.Precision.HIGHEST


def product(left, right):
    return jnp.dot(left, right, precision=precise, preferred_element_type=jnp.float32)


def inner_product(left, right):
    return lax.dot_general(
        left, right, (((0,), (0,)), ((), ())), precision=precise, preferred_element_type=jnp.float32
    )


def outer_product(left, right):
    return lax.dot_general(
        left, right, (((1,), (1,)), ((), ())), precision=precise, preferred_element_type=jnp.float32
    )


def tile_pattern(tile_mask, first_block, blocks):
    window = lax.dynamic_slice_in_dim(tile_mask, first_block, blocks, 1).astype(jnp.float32)
    window = jnp.transpose(window, (1, 0, 2))
    widened = jnp.broadcast_to(window[:, None, :, :, None], (blocks, BLK, SUPER, W // BLK, BLK))
    return widened.reshape(blocks * BLK, SUPER, W)


def row_term(anc_inverse, lower_cols):
    return product(anc_inverse, lower_cols)


def col_term(anc_inverse, upper_rows):
    return inner_product(anc_inverse, upper_rows)


def per_device(anc_inverse, lower_anc, upper_anc, lower_edge, upper_edge, diag_inverse, tile_mask):
    rows_here, cols_here = anc_inverse.shape
    slab_rows = rows_here // lax.axis_size("col")
    row_index = lax.axis_index("row")
    col_index = lax.axis_index("col")
    col_pattern = tile_pattern(tile_mask, col_index * (cols_here // BLK), cols_here // BLK)
    row_pattern = tile_pattern(tile_mask, row_index * (rows_here // BLK), rows_here // BLK)
    lower_list = []
    upper_list = []
    cols_list = []
    rows_list = []
    lower_full = lax.all_gather(lower_anc, "row", axis=2, tiled=True) * col_pattern
    upper_full = lax.all_gather(upper_anc, "col", axis=2, tiled=True) * row_pattern
    cols_all = lax.psum_scatter(
        row_term(anc_inverse, lower_full.reshape(cols_here, SUPER * W)),
        "col",
        scatter_dimension=0,
        tiled=True,
    )
    rows_all = lax.psum_scatter(
        col_term(anc_inverse, upper_full.reshape(rows_here, SUPER * W)),
        "row",
        scatter_dimension=0,
        tiled=True,
    )
    cols_all = cols_all.reshape(slab_rows, SUPER, W)
    rows_all = rows_all.reshape(slab_rows, SUPER, W)
    for node_index in range(SUPER):
        lower_list.append(lower_full[:, node_index, :])
        upper_list.append(upper_full[:, node_index, :])
        cols_list.append(cols_all[:, node_index, :])
        rows_list.append(rows_all[:, node_index, :])
    x_list = []
    y_list = []
    corner_list = []
    cross_cols = []
    cross_rows = []
    for node_index in range(SUPER):
        lower_cur = lower_list[node_index]
        upper_cur = upper_list[node_index]
        inv_cols = -cols_list[node_index]
        inv_rows = -rows_list[node_index]
        upper_mine = lax.dynamic_slice_in_dim(upper_cur, col_index * slab_rows, slab_rows, 0)
        if node_index > 0:
            lower_side = lower_edge[node_index - 1]
            upper_side = upper_edge[node_index - 1]
            lower_mine = lax.dynamic_slice_in_dim(lower_cur, row_index * slab_rows, slab_rows, 0)
            rows_lower = inner_product(prev_rows, lower_mine)
            upper_cols = inner_product(upper_mine, prev_cols)
        if node_index > 0:
            rows_lower, upper_cols = lax.psum((rows_lower, upper_cols), ("row", "col"))
        if node_index > 0:
            cross_col = -(rows_lower + product(prev_corner, lower_side))
            cross_row = -(upper_cols + product(upper_side, prev_corner))
            inv_cols = inv_cols - product(prev_cols, lower_side)
            inv_rows = inv_rows - outer_product(prev_rows, upper_side)
            cross_cols.append(cross_col)
            cross_rows.append(cross_row)
        inv_corner = diag_inverse[node_index] - lax.psum(
            inner_product(upper_mine, inv_cols), ("row", "col")
        )
        if node_index > 0:
            inv_corner = inv_corner - product(upper_side, cross_col)
        x_list.append(inv_cols)
        y_list.append(inv_rows)
        corner_list.append(inv_corner)
        prev_cols = inv_cols
        prev_rows = inv_rows
        prev_corner = inv_corner
    x_blocks = jnp.stack(x_list, axis=1)
    y_blocks = jnp.stack(y_list, axis=1)[None, None]
    tile_rows = W // lax.axis_size("row")
    tile_cols = W // lax.axis_size("col")
    corners = jnp.stack(corner_list)
    corners = lax.dynamic_slice_in_dim(corners, row_index * tile_rows, tile_rows, 1)
    z_blocks = lax.dynamic_slice_in_dim(corners, col_index * tile_cols, tile_cols, 2)
    crossed = jnp.stack([jnp.stack(cross_cols), jnp.stack(cross_rows)])
    crossed = lax.dynamic_slice_in_dim(crossed, row_index * tile_rows, tile_rows, 2)
    cross_blocks = lax.dynamic_slice_in_dim(crossed, col_index * tile_cols, tile_cols, 3)
    return (x_blocks, y_blocks, z_blocks, cross_blocks)


def solution(mesh):
    return jax.shard_map(
        per_device,
        mesh=mesh,
        in_specs=(
            P("row", "col"),
            P("col", None, "row"),
            P("row", None, "col"),
            P(),
            P(),
            P(),
            P(),
        ),
        out_specs=(
            P(("row", "col"), None, None),
            P("col", "row", None, None, None),
            P(None, "row", "col"),
            P(None, None, "row", "col"),
        ),
        check_vma=False,
    )
```

profile of v0, /device:TPU:0, one launch (start us, length us, event | category | flops | bytes accessed | tf_op | source)
XLA Modules:
  0.0 565.6 jit_solution(17613502817447202190)
XLA Ops:
  8.9 4.2 broadcast_in_dim.6
  13.1 10.5 %reshape.42 = f32[1280,3,384]{2,0,1:T(8,128)} reshape(f32[10,128,3,3,128]{4,3,1,0,2:T(4,128)} %broadcast_in_dim.6) | data formatting | bytes 11796480 | tf_op jit(solution)/shard_map/reshape | solution.py:32
  23.6 55.8 %all-gather.3.cloned.1.call-done = f32[1280,3,384]{0,2,1:T(8,128)} async-done(((f32[1280,3,96]{0,2,1:T(8,128)}), f32[1280,3,384]{0,2,1:T(8,128)}) %all-gather.3.cloned.1.call-update) | async-done | bytes 5898256 | tf_op jit(solution)/shard_map/all_gather | solution.py:54
  79.3 7.7 %copy.70 = f32[1280,3,384]{2,0,1:T(8,128)} copy(f32[1280,3,384]{0,2,1:T(8,128)} %all-gather.3.cloned.1.call-done) | data formatting | bytes 11796480 | tf_op jit(solution)/shard_map/all_gather | solution.py:54
  87.0 9.3 %mul.30 = f32[1280,3,384]{2,0,1:T(8,128)} multiply(f32[1280,3,384]{2,0,1:T(8,128)} %copy.70, f32[1280,3,384]{2,0,1:T(8,128)} %reshape.42) | non-fusion elementwise | flops 1474560 | bytes 17694720 | tf_op jit(solution)/shard_map/mul | solution.py:54
  96.3 7.8 %copy.71 = f32[1280,3,384]{0,2,1:T(8,128)} copy(f32[1280,3,384]{2,0,1:T(8,128)} %mul.30) | data formatting | bytes 11796480 | tf_op jit(solution)/shard_map/mul | solution.py:54
  104.0 52.7 %convolution_bitcast_fusion = f32[2560,1152]{0,1:T(8,128)} fusion(f32[1280,1152]{0,1:T(8,128)} %bitcast.163, f32[2560,1280]{1,0:T(8,128)} %param.7), kind=kOutput, calls=%fused_computation | convolution fusion | flops 45298483200 | bytes 30801920 | tf_op jit(solution)/shard_map/dot_general | solution.py:13
  156.8 13.6 %copy.92 = f32[2560,1152]{1,0:T(8,128)} copy(f32[2560,1152]{0,1:T(8,128)} %convolution_bitcast_fusion) | data formatting | bytes 23592960
  171.1 6.0 %broadcast_in_dim.7 = f32[20,128,3,3,128]{1,0,4,3,2:T(8,128)} broadcast(f32[20,3,3]{0,2,1:T(4,128)S(1)} %convert_bitcast_fusion), dimensions={0,2,3} | broadcast | bytes 11797200 | tf_op jit(solution)/shard_map/broadcast_in_dim | solution.py:31
  177.1 13.7 %reshape.45 = f32[2560,3,384]{0,2,1:T(8,128)} reshape(f32[20,128,3,3,128]{1,0,4,3,2:T(8,128)} %broadcast_in_dim.7) | data formatting | bytes 23592960 | tf_op jit(solution)/shard_map/reshape | solution.py:32
  191.2 9.7 %mul.32 = f32[2560,3,384]{0,2,1:T(8,128)S(1)} multiply(f32[2560,3,384]{0,2,1:T(8,128)} %all-gather.5.cloned.1.call-done, f32[2560,3,384]{0,2,1:T(8,128)} %reshape.45) | non-fusion elementwise | flops 2949120 | bytes 35389440 | tf_op jit(solution)/shard_map/mul | solution.py:55
  200.9 4.3 copy-done
  205.3 50.1 %convolution_bitcast_fusion.1 = f32[1280,1152]{0,1:T(8,128)} fusion(f32[2560,1152]{0,1:T(8,128)S(1)} %bitcast.157, f32[2560,1280]{1,0:T(8,128)} %param.7), kind=kOutput, calls=%fused_computation.1 | convolution fusion | flops 45298483200 | bytes 30801920 | tf_op jit(solution)/shard_map/dot_general | solution.py:17
  255.4 7.7 %copy.94 = f32[1280,1152]{1,0:T(8,128)} copy(f32[1280,1152]{0,1:T(8,128)} %convolution_bitcast_fusion.1) | data formatting | bytes 11796480
  263.3 4.3 fusion.75
  267.6 9.3 %fusion.74 = (f32[2560,1,384]{0,2,1:T(8,128)}, f32[2560,1,384]{0,2,1:T(8,128)}, f32[2560,1,384]{0,2,1:T(8,128)}) fusion(f32[2560,3,384]{0,2,1:T(8,128)} %copy-done), kind=kLoop, calls=%fused_computation.100 | loop fusion | bytes 23592960 | tf_op jit(solution)/shard_map/slice | solution.py:72
  276.9 36.6 %reduce-scatter.7.cloned.1.call-done = f32[320,1152]{1,0:T(8,128)} async-done(((f32[2560,1152]{1,0:T(8,128)}), f32[320,1152]{1,0:T(8,128)}) %reduce-scatter.7.cloned.1.call-update) | async-done | bytes 1474576
  313.5 2.1 copy.93
  319.1 3.3 fusion.16
  323.5 3.3 fusion.18
  326.7 3.3 fusion.12
  331.9 3.2 fusion.14
  335.1 46.5 %reduce-scatter.9.cloned.1.call-done = f32[320,1152]{1,0:T(8,128)} async-done(((f32[1280,1152]{1,0:T(8,128)}), f32[320,1152]{1,0:T(8,128)}) %reduce-scatter.9.cloned.1.call-update) | async-done | bytes 1474576
  381.6 2.3 copy.95
  386.6 2.1 copy.100
  388.7 3.3 fusion.20
  393.1 3.2 fusion.49
  396.3 3.2 fusion.47
  402.5 2.2 pad_maximum_fusion
  407.0 137.7 %all-reduce.3.cloned.1.call-done = (f32[384,384]{1,0:T(8,128)}, f32[384,384]{1,0:T(8,128)}, f32[384,384]{1,0:T(8,128)}, f32[384,384]{1,0:T(8,128)}, f32[384,384]...) async-done(((f32[384,384]{1,0:T(8,128)}, f32[384,384]{1,0:T(8,128)}, f32[384,384]{1,0:T(8,128)}, f32[384,384]{1,0:T(8,128)}, f32[384,384]{1,0:T(8,128)}, ...) | async-done | bytes 4128784 | tf_op jit(solution)/shard_map/psum | solution.py:101
  546.3 2.5 fusion.7
  555.4 2.5 fusion.9
  (71 shorter events, 27.2 us)
Async XLA Ops:
  7.2 1.5 copy-start.16
  7.2 72.2 %all-gather.3.cloned.1.call-start = ((), (), s32[]{:S(2)}) async-start(), calls=%async_computation.2 | async-start | bytes 7372800 | tf_op jit(solution)/shard_map/all_gather | solution.py:54
  7.9 183.3 %all-gather.5.cloned.1.call-start = ((), (), s32[]{:S(2)}) async-start(), calls=%async_computation.3 | async-start | bytes 13271040 | tf_op jit(solution)/shard_map/all_gather | solution.py:55
  8.7 304.8 %reduce-scatter.7.cloned.1.call-start = ((), (), s32[]{:S(2)}) async-start(), calls=%async_computation.4 | async-start | bytes 13271040
  170.4 211.2 %reduce-scatter.9.cloned.1.call-start = ((), (), s32[]{:S(2)}) async-start(), calls=%async_computation.5 | async-start | bytes 7372800
  200.9 4.3 copy-start
  263.1 281.6 %all-reduce.3.cloned.1.call-start = ((), (), s32[]{:S(2)}) async-start(), calls=%async_computation.6 | async-start | bytes 8257536 | tf_op jit(solution)/shard_map/psum | solution.py:101
  317.8 4.5 copy-start.4
  319.1 3.3 copy-start.9
  331.1 0.8 copy-start.6
  385.2 6.8 %copy-start.1 = (f32[2,384,384]{2,1,0:T(8,128)S(1)}, f32[2,384,384]{2,1,0:T(8,128)}, u32[]{:S(2)}) copy-start(f32[2,384,384]{2,1,0:T(8,128)} %param.11) | copy-start | bytes 3538948
  388.7 3.3 copy-start.10
  400.4 2.1 copy-start.7
  404.7 1.1 copy-start.8
  544.7 1.5 copy-start.2
  544.7 1.6 copy-start.15
  544.7 4.2 copy-start.14
  546.1 2.7 copy-start.3
  546.1 2.7 copy-start.5
  548.8 1.3 copy-start.13
  550.1 1.3 copy-start.12
  551.5 1.6 copy-start.11
Sparse Core Ops, SparseCore 0:
  9.8 69.4 all-gather.2
  81.0 110.1 all-gather.4
  193.5 119.9 reduce-scatter.6
  316.4 65.2 reduce-scatter.8
  399.6 144.9 all-reduce.2
where the time goes:
time: 574 us; the launch traced here: 566 us
  waiting for transfers between devices  278 us (48%)
  matrix products  140 us (24%)
  local copies, waits for them, and re-layouts  105 us (18%)
  other arithmetic  26.1 us (5%)
  between operations  14.4 us (3%)
    psum x1, waiting for transfers between devices, per_device(): lax.psum(inner_product(upper_mine, inv_cols), ('row', 'col'))  138 us
    unnamed x7, waiting for transfers between devices  84.6 us
    dot_general x8, matrix products, inner_product(): lax.dot_general(left, right, (((0,), (0,)), ((), ())), precision=precise,...  72.9 us
    dot_general x9, matrix products, product(): jnp.dot(left, right, precision=precise, preferred_element_type=jnp.float32)  65.3 us
    all_gather x1, waiting for transfers between devices, per_device(): lax.all_gather(lower_anc, 'row', axis=2, tiled=True) * col_pattern  55.8 us
    unnamed x46, local copies, waits for them, and re-layouts  39.8 us
    reshape x2, local copies, waits for them, and re-layouts, tile_pattern(): return widened.reshape(blocks * BLK, SUPER, W)  24.2 us
  transfers between devices with their start and end apart: 5, of which 5 were waited for; matrix products, arithmetic and copies ran while one was open for 42% of the time, Pallas kernels for 0%

commit v1 on v0

--- a/solution.py
+++ b/solution.py
@@ -99,7 +99,7 @@
             cross_cols.append(cross_col)
             cross_rows.append(cross_row)
         inv_corner = diag_inverse[node_index] - lax.psum(
-            inner_product(upper_mine, inv_cols), ("row", "col")
+            lax.psum(inner_product(upper_mine, inv_cols), "row"), "col"
         )
         if node_index > 0:
             inv_corner = inv_corner - product(upper_side, cross_col)

time: 574 us -> 686 us (1.20)
  waiting for transfers between devices: 278 us -> 388 us
    psum x1 -> x3, waiting for transfers between devices: 138 us -> 245 us  [the longest x1 140 us: per_device(): rows_lower, upper_cols = lax.psum((rows_lower, upper_cols), ('row', 'col'))]
    unnamed x7 -> x9, waiting for transfers between devices: 84.6 us -> 86.7 us
    unnamed x46 -> x48, local copies, waits for them, and re-layouts: 39.8 us -> 40.2 us
  transfers between devices with their start and end apart: 5 -> 7, of which waited for: 5 -> 7; matrix products, arithmetic and copies ran while one was open for 42% -> 38% of each run, Pallas kernels for 0% -> 0%
where the time goes in v1:
time: 686 us; the launch traced here: 678 us
  waiting for transfers between devices  388 us (57%)
  matrix products  142 us (21%)
  local copies, waits for them, and re-layouts  106 us (15%)
  other arithmetic  26.8 us (4%)
  between operations  14.7 us (2%)
    psum x1, waiting for transfers between devices, per_device(): rows_lower, upper_cols = lax.psum((rows_lower, upper_cols), ('row', 'col'))  140 us
    unnamed x9, waiting for transfers between devices  86.7 us
    dot_general x8, matrix products, inner_product(): lax.dot_general(left, right, (((0,), (0,)), ((), ())), precision=precise,...  72.9 us
    dot_general x9, matrix products, product(): jnp.dot(left, right, precision=precise, preferred_element_type=jnp.float32)  66.6 us
    psum x1, waiting for transfers between devices, per_device(): lax.psum(inner_product(upper_mine, inv_cols), 'row')  60.7 us
    all_gather x1, waiting for transfers between devices, per_device(): lax.all_gather(lower_anc, 'row', axis=2, tiled=True) * col_pattern  55.8 us
    psum x1, waiting for transfers between devices, per_device(): lax.psum(lax.psum(inner_product(upper_mine, inv_cols), 'row'), 'col')  43.7 us
    unnamed x48, local copies, waits for them, and re-layouts  40.2 us
  transfers between devices with their start and end apart: 7, of which 7 were waited for; matrix products, arithmetic and copies ran while one was open for 38% of the time, Pallas kernels for 0%

profile of v1, /device:TPU:0, one launch (start us, length us, event | category | flops | bytes accessed | tf_op | source)
XLA Modules:
  0.0 678.1 jit_solution(10047596744527097252)
XLA Ops:
  8.9 4.1 broadcast_in_dim.6
  13.1 10.5 %reshape.42 = f32[1280,3,384]{2,0,1:T(8,128)} reshape(f32[10,128,3,3,128]{4,3,1,0,2:T(4,128)} %broadcast_in_dim.6) | data formatting | bytes 11796480 | tf_op jit(solution)/shard_map/reshape | solution.py:32
  23.5 55.8 %all-gather.3.cloned.1.call-done = f32[1280,3,384]{0,2,1:T(8,128)} async-done(((f32[1280,3,96]{0,2,1:T(8,128)}), f32[1280,3,384]{0,2,1:T(8,128)}) %all-gather.3.cloned.1.call-update) | async-done | bytes 5898256 | tf_op jit(solution)/shard_map/all_gather | solution.py:54
  79.3 7.7 %copy.70 = f32[1280,3,384]{2,0,1:T(8,128)} copy(f32[1280,3,384]{0,2,1:T(8,128)} %all-gather.3.cloned.1.call-done) | data formatting | bytes 11796480 | tf_op jit(solution)/shard_map/all_gather | solution.py:54
  87.0 9.3 %mul.30 = f32[1280,3,384]{2,0,1:T(8,128)} multiply(f32[1280,3,384]{2,0,1:T(8,128)} %copy.70, f32[1280,3,384]{2,0,1:T(8,128)} %reshape.42) | non-fusion elementwise | flops 1474560 | bytes 17694720 | tf_op jit(solution)/shard_map/mul | solution.py:54
  96.3 7.8 %copy.71 = f32[1280,3,384]{0,2,1:T(8,128)} copy(f32[1280,3,384]{2,0,1:T(8,128)} %mul.30) | data formatting | bytes 11796480 | tf_op jit(solution)/shard_map/mul | solution.py:54
  104.0 52.7 %convolution_bitcast_fusion = f32[2560,1152]{0,1:T(8,128)} fusion(f32[1280,1152]{0,1:T(8,128)} %bitcast.163, f32[2560,1280]{1,0:T(8,128)} %param.7), kind=kOutput, calls=%fused_computation | convolution fusion | flops 45298483200 | bytes 30801920 | tf_op jit(solution)/shard_map/dot_general | solution.py:13
  156.7 13.6 %copy.92 = f32[2560,1152]{1,0:T(8,128)} copy(f32[2560,1152]{0,1:T(8,128)} %convolution_bitcast_fusion) | data formatting | bytes 23592960
  171.0 6.0 broadcast_in_dim.7
  177.0 13.7 %reshape.45 = f32[2560,3,384]{0,2,1:T(8,128)} reshape(f32[20,128,3,3,128]{1,0,4,3,2:T(8,128)} %broadcast_in_dim.7) | data formatting | bytes 23592960 | tf_op jit(solution)/shard_map/reshape | solution.py:32
  191.2 9.7 %mul.32 = f32[2560,3,384]{0,2,1:T(8,128)S(1)} multiply(f32[2560,3,384]{0,2,1:T(8,128)} %all-gather.5.cloned.1.call-done, f32[2560,3,384]{0,2,1:T(8,128)} %reshape.45) | non-fusion elementwise | flops 2949120 | bytes 35389440 | tf_op jit(solution)/shard_map/mul | solution.py:55
  200.9 4.3 copy-done
  205.3 50.1 %convolution_bitcast_fusion.1 = f32[1280,1152]{0,1:T(8,128)} fusion(f32[2560,1152]{0,1:T(8,128)S(1)} %bitcast.157, f32[2560,1280]{1,0:T(8,128)} %param.7), kind=kOutput, calls=%fused_computation.1 | convolution fusion | flops 45298483200 | bytes 30801920 | tf_op jit(solution)/shard_map/dot_general | solution.py:17
  255.4 7.7 %copy.94 = f32[1280,1152]{1,0:T(8,128)} copy(f32[1280,1152]{0,1:T(8,128)} %convolution_bitcast_fusion.1) | data formatting | bytes 11796480
  263.3 9.2 %fusion.74 = (f32[2560,1,384]{0,2,1:T(8,128)}, f32[2560,1,384]{0,2,1:T(8,128)}, f32[2560,1,384]{0,2,1:T(8,128)}) fusion(f32[2560,3,384]{0,2,1:T(8,128)} %copy-done), kind=kLoop, calls=%fused_computation.100 | loop fusion | bytes 23592960 | tf_op jit(solution)/shard_map/slice | solution.py:72
  272.6 40.9 %reduce-scatter.7.cloned.1.call-done = f32[320,1152]{1,0:T(8,128)} async-done(((f32[2560,1152]{1,0:T(8,128)}), f32[320,1152]{1,0:T(8,128)}) %reduce-scatter.7.cloned.1.call-update) | async-done | bytes 1474576
  319.8 3.3 fusion.20
  324.2 3.3 fusion.18
  329.3 3.3 fusion.14
  332.7 4.6 fusion.75
  337.3 44.4 %reduce-scatter.9.cloned.1.call-done = f32[320,1152]{1,0:T(8,128)} async-done(((f32[1280,1152]{1,0:T(8,128)}), f32[320,1152]{1,0:T(8,128)}) %reduce-scatter.9.cloned.1.call-update) | async-done | bytes 1474576
  383.8 3.3 fusion.12
  388.3 60.7 %all-reduce.11.cloned.1.call-done = (f32[384,384]{1,0:T(8,128)}, f32[384,384]{1,0:T(8,128)}, f32[384,384]{1,0:T(8,128)}) async-done(((f32[384,384]{1,0:T(8,128)}, f32[384,384]{1,0:T(8,128)}, f32[384,384]{1,0:T(8,128)}), (f32[384,384]{1,0:T(8,128)}, f32[384,384]{1,0:T(8,128)}, f32[384,384]{1,0:T(8,128)})) %all-reduce.11.cloned.1.call-update) | async-done | bytes 1769488 | tf_op jit(solution)/shard_map/psum | solution.py:102
  449.3 3.3 fusion.16
  456.0 3.3 fusion.49
  460.4 3.2 fusion.47
  466.6 2.2 pad_maximum_fusion
  471.1 43.7 %all-reduce.9.cloned.1.call-done = (f32[384,384]{1,0:T(8,128)}, f32[384,384]{1,0:T(8,128)}, f32[384,384]{1,0:T(8,128)}) async-done(((f32[384,384]{1,0:T(8,128)}, f32[384,384]{1,0:T(8,128)}, f32[384,384]{1,0:T(8,128)}), (f32[384,384]{1,0:T(8,128)}, f32[384,384]{1,0:T(8,128)}, f32[384,384]{1,0:T(8,128)})) %all-reduce.9.cloned.1.call-update) | async-done | bytes 1769488 | tf_op jit(solution)/shard_map/psum | solution.py:101
  517.0 140.0 %all-reduce.7.cloned.1.call-done = (f32[384,384]{1,0:T(8,128)}, f32[384,384]{1,0:T(8,128)}, f32[384,384]{1,0:T(8,128)}, f32[384,384]{1,0:T(8,128)}) async-done(((f32[384,384]{1,0:T(8,128)}, f32[384,384]{1,0:T(8,128)}, f32[384,384]{1,0:T(8,128)}, f32[384,384]{1,0:T(8,128)}), (f32[384,384]{1,0:T(8,128)}, f32[384,384]{1,0:T(8,128)}, f32[384,384]{1,0:T(8,128)}, ...) | async-done | bytes 2359312 | tf_op jit(solution)/shard_map/psum | solution.py:93
  657.1 2.7 fusion.7
  659.8 2.4 fusion
  667.6 2.5 fusion.9
  (79 shorter events, 34.1 us)
Async XLA Ops:
  7.2 1.5 copy-start.17
  7.2 72.2 %all-gather.3.cloned.1.call-start = ((), (), s32[]{:S(2)}) async-start(), calls=%async_computation.2 | async-start | bytes 7372800 | tf_op jit(solution)/shard_map/all_gather | solution.py:54
  7.9 183.3 %all-gather.5.cloned.1.call-start = ((), (), s32[]{:S(2)}) async-start(), calls=%async_computation.3 | async-start | bytes 13271040 | tf_op jit(solution)/shard_map/all_gather | solution.py:55
  8.7 304.8 %reduce-scatter.7.cloned.1.call-start = ((), (), s32[]{:S(2)}) async-start(), calls=%async_computation.4 | async-start | bytes 13271040
  170.3 211.3 %reduce-scatter.9.cloned.1.call-start = ((), (), s32[]{:S(2)}) async-start(), calls=%async_computation.5 | async-start | bytes 7372800
  200.9 4.3 copy-start
  263.1 185.9 %all-reduce.11.cloned.1.call-start = ((), (), s32[]{:S(2)}) async-start(), calls=%async_computation.8 | async-start | bytes 3538944 | tf_op jit(solution)/shard_map/psum | solution.py:102
  317.8 5.3 copy-start.4
  318.8 4.3 copy-start.11
  323.1 4.3 copy-start.12
  328.5 0.8 copy-start.7
  332.6 182.2 %all-reduce.9.cloned.1.call-start = ((), (), s32[]{:S(2)}) async-start(), calls=%async_computation.7 | async-start | bytes 3538944 | tf_op jit(solution)/shard_map/psum | solution.py:101
  449.1 208.0 %all-reduce.7.cloned.1.call-start = ((), (), s32[]{:S(2)}) async-start(), calls=%async_computation.6 | async-start | bytes 4718592 | tf_op jit(solution)/shard_map/psum | solution.py:93
  452.6 6.8 copy-start.1
  456.0 3.3 copy-start.13
  464.5 2.1 copy-start.8
  468.8 1.1 copy-start.10
  514.9 142.2 %copy-start.2 = (f32[384,384]{1,0:T(8,128)S(1)}, f32[384,384]{1,0:T(8,128)}, u32[]{:S(2)}) copy-start(f32[384,384]{1,0:T(8,128)} %get-tuple-element.28) | copy-start | bytes 1769476
  517.0 142.8 %copy-start.5 = (f32[2,384,384]{2,1,0:T(8,128)S(1)}, f32[2,384,384]{2,1,0:T(8,128)}, u32[]{:S(2)}) copy-start(f32[2,384,384]{2,1,0:T(8,128)} %param.10) | copy-start | bytes 3538948
  657.1 2.7 copy-start.3
  659.8 2.4 copy-start.14
  662.2 1.4 copy-start.16
  663.6 1.6 copy-start.6
  663.6 1.6 copy-start.15
  666.8 3.3 copy-start.9
Sparse Core Ops, SparseCore 0:
  9.8 69.4 all-gather.2
  81.0 110.1 all-gather.4
  193.5 119.9 reduce-scatter.6
  316.4 65.2 reduce-scatter.8
  384.9 64.0 all-reduce.10
  451.5 63.3 all-reduce.8
  520.9 136.1 all-reduce.6
